TPU v7x, 32 devices: a whole 2x2x4 slice. The times are simulated.
32 devices in a mesh: dp: 8 (over z, y), hg: 2 (over x), hid: 2 (over core).
Axes of the slice: x: 2, y: 2, z: 4, core: 2. Of those that a mesh axis runs over, the one named last changes fastest.
Arguments:
- tokens: bfloat16 [18816, 768], P(('dp', 'hid')), may hold values from -6 to 6
- big_images: int32 [16], P(('dp', 'hid')), may hold values from 0 to 1, as said below
- norm_gain: bfloat16 [768], replicated, may hold values from 0.5 to 1.5
- w_qkv: bfloat16 [768, 2304], P(None, 'hg'), may hold values from -0.21875 to 0.21875
- qk_gains: bfloat16 [2, 64], replicated, may hold values from 0.099609375 to 1.8984375
- w_out_t: bfloat16 [768, 768], P(None, 'hg'), may hold values from -0.625 to 0.625
- w_in: bfloat16 [768, 3072], P(None, ('hg', 'hid')), may hold values from -0.21875 to 0.21875
- w_back: bfloat16 [768, 3072], P(None, ('hg', 'hid')), may hold values from -0.109375 to 0.109375
- cotangent: bfloat16 [18816, 768], P(('dp', 'hid'), 'hg'), may hold values from -6 to 6
Outputs:
- output: bfloat16 [18816, 768], P(('dp', 'hid'), 'hg')
- token_grad: bfloat16 [18816, 768], P(('dp', 'hid'))
- norm_gain_grad: float32 [768], P(('dp', 'hid'))
- w_qkv_grad: float32 [768, 2304], P(('dp', 'hid'), 'hg')
- qk_gains_grad: float32 [2, 64], replicated
- w_out_t_grad: float32 [768, 768], P(('dp', 'hid'), 'hg')
- w_in_grad: float32 [768, 3072], P('dp', ('hg', 'hid'))
- w_back_grad: float32 [768, 3072], P('dp', ('hg', 'hid'))
Inputs may be any that keep to these rules, and one draw needn't show every extreme that they name: `big_images`: 1 where the 1176 tokens of a group form one image, 0 where they form 6 images of 196 tokens each in order; every draw has groups of both kinds.
All inputs are finite; a program needn't handle non-finite values.
Results may differ from a plain program's by a relative error of at most 0.012.
Values may be sent and summed in bfloat16 or wider, within the bound.
No kernel may reach another device: no remote copies, remote signals or barrier semaphores. Data moves between devices by JAX's collectives and lax.ppermute only.
A program may use at most 256 MiB of HBM per device.

v0:
```python
import jax
import jax.numpy as jnp
from jax import lax
from jax.sharding import PartitionSpec as P

PATCHES = 196
EPSILON = 1e-06


def normalize(values):
    centred = values - jnp.mean(values, axis=-1, keepdims=True)
    inverse = lax.rsqrt(jnp.mean(centred * centred, axis=-1, keepdims=True) + EPSILON)
    return (centred * inverse, inverse)


def normalize_back(upstream, normed, inverse):
    inner = jnp.mean(upstream * normed, axis=-1, keepdims=True)
    return inverse * (upstream - jnp.mean(upstream, axis=-1, keepdims=True) - normed * inner)


def times_t(left, right):
    return lax.dot_general(
        left, right, (((1,), (1,)), ((), ())), preferred_element_type=jnp.float32
    )


def rows_t(left, right):
    return lax.dot_general(
        left, right, (((0,), (0,)), ((), ())), preferred_element_type=jnp.float32
    )


def masked_scores(queries, keys_in, allowed):
    scores = jnp.einsum("gqe,gke->gqk", queries, keys_in, preferred_element_type=jnp.float32)
    return jnp.where(allowed, scores, -1e30)


def head_forward(queries, keys_in, values_in, allowed):
    scores = masked_scores(queries, keys_in, allowed)
    highest = jnp.max(scores, axis=-1, keepdims=True)
    expo_scores = jnp.exp(scores - highest)
    totals = jnp.sum(expo_scores, axis=-1, keepdims=True)
    weights = (expo_scores / totals).astype(jnp.bfloat16)
    attended = jnp.einsum("gqk,gke->gqe", weights, values_in, preferred_element_type=jnp.float32)
    return (attended, (highest + jnp.log(totals))[..., 0])


def head_back(queries, keys_in, values_in, log_total, grad_out, allowed):
    scores = masked_scores(queries, keys_in, allowed)
    probs = jnp.exp(scores - log_total[..., None])
    grad_probs = jnp.einsum("gqe,gke->gqk", grad_out, values_in, preferred_element_type=jnp.float32)
    inner = jnp.sum(grad_probs * probs, axis=-1, keepdims=True)
    grad_scores = (probs * (grad_probs - inner)).astype(jnp.bfloat16)
    grad_values = jnp.einsum(
        "gqk,gqe->gke", probs.astype(jnp.bfloat16), grad_out, preferred_element_type=jnp.float32
    )
    grad_queries = jnp.einsum(
        "gqk,gke->gqe", grad_scores, keys_in, preferred_element_type=jnp.float32
    )
    grad_keys = jnp.einsum("gqk,gqe->gke", grad_scores, queries, preferred_element_type=jnp.float32)
    return (grad_queries, grad_keys, grad_values)


def attention_pass(step_fn, arrays, big_flag):
    heads_here = arrays[0].shape[0]
    tok_rows = arrays[0].shape[1]
    image_of = jnp.arange(tok_rows) // PATCHES
    allowed = (image_of[:, None] == image_of[None, :]) | (big_flag > 0)
    run_allowed = allowed[None]
    shaped = tuple(
        (member.reshape((heads_here, 1, tok_rows // 1) + member.shape[2:]) for member in arrays)
    )
    results = lax.map(lambda blocks: step_fn(*blocks, run_allowed), shaped)
    return tuple((member.reshape((heads_here, tok_rows) + member.shape[3:]) for member in results))


def shards(tokens, big_images, norm_gain, w_qkv, qk_gains, w_out_t, w_in, w_back, cotangent):
    tok_rows = tokens.shape[0]
    width = tokens.shape[1]
    head_size = qk_gains.shape[1]
    heads_here = w_qkv.shape[1] // (3 * head_size)
    half_width = heads_here * head_size
    big_flag = big_images[0]
    head_scale = head_size ** (-0.5)
    inputs = tokens.astype(jnp.float32)
    normed, inverse = normalize(inputs)
    gain_vec = norm_gain.astype(jnp.float32)
    normed_low = (normed * gain_vec).astype(jnp.bfloat16)
    joined = jnp.dot(normed_low, w_qkv, preferred_element_type=jnp.float32).reshape(
        tok_rows, heads_here, 3, head_size
    )
    q_hat, q_inverse = normalize(joined[:, :, 0])
    k_hat, k_inverse = normalize(joined[:, :, 1])
    q_gain = qk_gains[0].astype(jnp.float32)
    k_gain = qk_gains[1].astype(jnp.float32)
    queries = (q_hat * q_gain * head_scale).astype(jnp.bfloat16).transpose(1, 0, 2)
    keys_in = (k_hat * k_gain).astype(jnp.bfloat16).transpose(1, 0, 2)
    values_in = joined[:, :, 2].astype(jnp.bfloat16).transpose(1, 0, 2)
    attended, log_total = attention_pass(head_forward, (queries, keys_in, values_in), big_flag)
    attended_low = attended.astype(jnp.bfloat16).transpose(1, 0, 2).reshape(tok_rows, half_width)
    attn_part = times_t(attended_low, w_out_t)
    normed_all = lax.all_gather(normed_low, "hid", axis=0, tiled=True)
    hidden_pre = jnp.dot(normed_all, w_in, preferred_element_type=jnp.float32)
    hidden_act = jax.nn.gelu(hidden_pre).astype(jnp.bfloat16)
    mlp_part = lax.psum_scatter(
        times_t(hidden_act, w_back).astype(jnp.bfloat16), "hid", scatter_dimension=0, tiled=True
    ).astype(jnp.float32)
    mixed = lax.psum_scatter(attn_part + mlp_part, "hg", scatter_dimension=1, tiled=True)
    out_cols = width // lax.axis_size("hg")
    input_cols = lax.dynamic_slice_in_dim(inputs, lax.axis_index("hg") * out_cols, out_cols, 1)
    output = (input_cols + mixed).astype(jnp.bfloat16)
    grad_out = lax.all_gather(cotangent, "hg", axis=1, tiled=True)
    grad_w_out = rows_t(grad_out, attended_low)
    grad_attended = jnp.dot(grad_out, w_out_t, preferred_element_type=jnp.float32)
    grad_att_low = (
        grad_attended.astype(jnp.bfloat16)
        .reshape(tok_rows, heads_here, head_size)
        .transpose(1, 0, 2)
    )
    grad_queries, grad_keys, grad_values = attention_pass(
        head_back, (queries, keys_in, values_in, log_total, grad_att_low), big_flag
    )
    grad_query = grad_queries.transpose(1, 0, 2) * head_scale
    grad_key = grad_keys.transpose(1, 0, 2)
    qk_partial = jnp.stack(
        [jnp.sum(grad_query * q_hat, axis=(0, 1)), jnp.sum(grad_key * k_hat, axis=(0, 1))]
    )
    grad_q_raw = normalize_back(grad_query * q_gain, q_hat, q_inverse)
    grad_k_raw = normalize_back(grad_key * k_gain, k_hat, k_inverse)
    grad_joined = jnp.stack([grad_q_raw, grad_k_raw, grad_values.transpose(1, 0, 2)], axis=2)
    grad_joined = grad_joined.reshape(tok_rows, 3 * half_width).astype(jnp.bfloat16)
    grad_w_qkv = rows_t(normed_low, grad_joined)
    grad_normed_att = times_t(grad_joined, w_qkv)
    grad_out_all = lax.all_gather(grad_out, "hid", axis=0, tiled=True)
    grad_act = jnp.dot(grad_out_all, w_back, preferred_element_type=jnp.float32)
    grad_up = jax.vjp(jax.nn.gelu, hidden_pre)[1](grad_act)[0].astype(jnp.bfloat16)
    grad_w_back = rows_t(grad_out_all, hidden_act)
    grad_w_in = rows_t(normed_all, grad_up)
    grad_normed_mlp = lax.psum_scatter(
        times_t(grad_up, w_in).astype(jnp.bfloat16), "hid", scatter_dimension=0, tiled=True
    ).astype(jnp.float32)
    grad_normed = lax.psum(grad_normed_att + grad_normed_mlp, "hg")
    token_grad = (
        normalize_back(grad_normed * gain_vec, normed, inverse) + grad_out.astype(jnp.float32)
    ).astype(jnp.bfloat16)
    gain_partial = jnp.sum(grad_normed * normed, axis=0)
    w_qkv_grad, w_out_t_grad, norm_gain_grad = (
        lax.psum_scatter(grad_w_qkv, ("dp", "hid"), scatter_dimension=0, tiled=True),
        lax.psum_scatter(grad_w_out, ("dp", "hid"), scatter_dimension=0, tiled=True),
        lax.psum_scatter(gain_partial, ("dp", "hid"), scatter_dimension=0, tiled=True),
    )
    w_in_grad, w_back_grad = (
        lax.psum_scatter(
            grad_w_in.astype(jnp.bfloat16), "dp", scatter_dimension=0, tiled=True
        ).astype(jnp.float32),
        lax.psum_scatter(
            grad_w_back.astype(jnp.bfloat16), "dp", scatter_dimension=0, tiled=True
        ).astype(jnp.float32),
    )
    qk_gains_grad = lax.psum(qk_partial, ("dp", "hg", "hid"))
    return (
        output,
        token_grad,
        norm_gain_grad,
        w_qkv_grad,
        qk_gains_grad,
        w_out_t_grad,
        w_in_grad,
        w_back_grad,
    )


def solution(mesh):
    return jax.shard_map(
        shards,
        mesh=mesh,
        in_specs=(
            P(("dp", "hid"), None),
            P(("dp", "hid")),
            P(),
            P(None, "hg"),
            P(),
            P(None, "hg"),
            P(None, ("hg", "hid")),
            P(None, ("hg", "hid")),
            P(("dp", "hid"), "hg"),
        ),
        out_specs=(
            P(("dp", "hid"), "hg"),
            P(("dp", "hid"), None),
            P(("dp", "hid")),
            P(("dp", "hid"), "hg"),
            P(),
            P(("dp", "hid"), "hg"),
            P("dp", ("hg", "hid")),
            P("dp", ("hg", "hid")),
        ),
        check_vma=False,
    )
```

profile of v0, /device:TPU:0, one launch (start us, length us, event | category | flops | bytes accessed | tf_op | source)
XLA Modules:
  0.0 659.5 jit_solution(1568707283787377378)
XLA Ops:
  8.0 34.2 %all-gather.6.cloned.1.call-done = bf16[1176,768]{1,0:T(8,128)(2,1)} async-done(((bf16[1176,384]{1,0:T(8,128)(2,1)}), bf16[1176,768]{1,0:T(8,128)(2,1)}) %all-gather.6.cloned.1.call-update) | async-done | bytes 1806352 | tf_op jit(solution)/shard_map/all_gather | solution.py:112
  48.1 4.0 fusion.76
  71.0 8.3 %fusion.77 = f32[2352,768]{1,0:T(8,128)} fusion(bf16[2352,768]{1,0:T(8,128)(2,1)} %all-gather.8.cloned.1.call-done, bf16[768,768]{1,0:T(8,128)(2,1)} %param.20), kind=kOutput, calls=%fused_computation.143 | convolution fusion | flops 2774532096 | bytes 12017664 | tf_op jit(solution)/shard_map/dot_general | solution.py:135
  79.3 11.3 %fusion.54 = (bf16[2352,768]{1,0:T(8,128)(2,1)S(1)}, f32[2352,768]{1,0:T(8,128)}) fusion(f32[2352,768]{1,0:T(8,128)} %fusion.77, bf16[2352,768]{1,0:T(8,128)(2,1)} %all-gather.4.cloned.1.call-done, bf16[768,768]{1,0:T(8,128)(2,1)} %param.19), kind=kOutput, calls=%fused_computation.61 | convolution fusion | flops 2810658816 | bytes 22855680 | tf_op jit(solution)/shard_map/dot_general | solution.py:103
  92.5 4.6 convolution_convert_fusion
  98.3 33.6 %while.30 = (s32[]{:T(128)}, bf16[6,1,1176,64]{2,3,1,0:T(8,128)(2,1)S(1)}, f32[6,1,1176]{2,1,0:T(1,128)S(1)}, bf16[6,1,1176,64]{3,2,1,0:T(8,128)(2,1)}, bf16[6,1...) while((s32[]{:T(128)}, ...), condition=%wide.region_9.10_spmd.clone.clone, body=%wide.region_6.9_spmd.clone.sunk.clone | while | flops 366487456 | bytes 18392728 | solution.py:73
  138.2 9.6 %convolution_convert_fusion.1 = bf16[2352,768]{1,0:T(8,128)(2,1)} fusion(bf16[768,768]{1,0:T(8,128)(2,1)} %param.20, f32[2352,768]{1,0:T(8,128)} %get-tuple-element.296), kind=kOutput, calls=%fused_computation.64 | convolution fusion | flops 2792595456 | bytes 12017664 | tf_op jit(solution)/shard_map/dot_general | solution.py:22
  149.1 79.0 %while.31 = (s32[]{:T(128)}, f32[6,1,1176,64]{2,3,1,0:T(8,128)}, f32[6,1,1176,64]{2,3,1,0:T(8,128)}, bf16[6,1,1176,64]{2,3,1,0:T(8,128)(2,1)S(1)}, bf16[6,1,1176...) while((s32[]{:T(128)}, f32[6,1,1176,64]{2,3,1,0:T(8,128)}, ...), condition=%wide.region_14.15_spmd.clone.clone, body=%wide.region_12.14_spmd.clone.sunk.clone | while | flops 898933184 | bytes 44843632 | solution.py:73
  228.0 9.3 %fusion.64 = bf16[768,768]{0,1:T(8,128)(2,1)} fusion(bf16[2352,768]{1,0:T(8,128)(2,1)} %all-gather.8.cloned.1.call-done, f32[2352,768]{1,0:T(8,128)} %get-tuple-element.296), kind=kOutput, calls=%fused_computation.109 | convolution fusion | flops 2791378944 | bytes 12017664 | tf_op jit(solution)/shard_map/dot_general | solution.py:28
  240.3 5.5 fusion.56
  247.7 4.4 convolution_convert_fusion.4
  253.8 4.1 fusion.68
  260.2 7.0 %convolution_add_fusion.1 = f32[1176,768]{1,0:T(8,128)} fusion(bf16[1176,1152]{0,1:T(8,128)(2,1)} %bitcast.277, bf16[768,1152]{1,0:T(8,128)(2,1)S(1)} %copy-done, bf16[1176,768]{1,0:T(8,128)(2,1)} %reduce-scatter.16.cloned.1.call-done), kind=kOutput, calls=%fused_computation.66 | convolution fusion | flops 2082705408 | bytes 9897984 | tf_op jit(solution)/shard_map/dot_general | solution.py:22
  268.5 4.5 convolution_add_fusion
  279.4 6.9 %fusion.78 = f32[768,1152]{1,0:T(8,128)} fusion(bf16[1176,768]{1,0:T(8,128)(2,1)} %multiply_convert_fusion.2, bf16[1176,1152]{0,1:T(8,128)(2,1)} %bitcast.278), kind=kOutput, calls=%fused_computation.144 | convolution fusion | flops 2080899072 | bytes 8054784 | tf_op jit(solution)/shard_map/dot_general | solution.py:28
  291.4 40.1 %psum.15 = f32[2,64]{1,0:T(2,128)} all-reduce(f32[2,64]{1,0:T(2,128)S(1)} %pad_maximum_fusion.1), channel_id=1, replica_groups=mesh['dp'=8,'hg'=2,'hid'=2] {'dp','hg','hid'}, use_global_device_ids=true, to_apply=%region_28.29 | all-reduce | flops 128 | bytes 1024 | tf_op jit(solution)/shard_map/psum | solution.py:160
  333.4 37.4 %reduce-scatter.20.cloned.1.call-done = bf16[96,768]{1,0:T(8,128)(2,1)} async-done(((bf16[768,768]{1,0:T(8,128)(2,1)}), bf16[96,768]{1,0:T(8,128)(2,1)}) %reduce-scatter.20.cloned.1.call-update) | async-done | bytes 147472 | tf_op jit(solution)/shard_map/reduce_scatter | solution.py:153
  372.5 95.6 %all-reduce.3.cloned.1.call-done = f32[1176,768]{1,0:T(8,128)} async-done(((f32[1176,768]{1,0:T(8,128)}), f32[1176,768]{1,0:T(8,128)}) %all-reduce.3.cloned.1.call-update) | async-done | bytes 3612688 | tf_op jit(solution)/shard_map/psum | solution.py:142
  468.1 4.1 multiply_reduce_fusion.1
  472.2 33.2 %all-reduce = f32[768]{0:T(1024)S(1)} all-reduce(f32[768]{0:T(1024)S(1)} %get-tuple-element.240), channel_id=5, replica_groups=mesh['dp'=8,'hg'=2,'hid'=2] {'dp','hid'}, use_global_device_ids=true, to_apply=%region_24.25.clone | all-reduce | flops 768 | bytes 6144
  506.0 4.7 add_convert_fusion
  510.7 8.4 %reduce-scatter.14.cloned.1.call-done = f32[1176,384]{1,0:T(8,128)} async-done(((f32[1176,768]{1,0:T(8,128)}), f32[1176,384]{1,0:T(8,128)}) %reduce-scatter.14.cloned.1.call-update) | async-done | bytes 1806352 | tf_op jit(solution)/shard_map/reduce_scatter | solution.py:108
  522.2 58.9 %reduce-scatter.22.cloned.1.call-done = f32[48,384]{1,0:T(8,128)} async-done(((f32[768,384]{1,0:T(8,128)}), f32[48,384]{1,0:T(8,128)}) %reduce-scatter.22.cloned.1.call-update) | async-done | bytes 73744
  581.1 71.6 %reduce-scatter.18.cloned.1.call-done = f32[48,1152]{1,0:T(8,128)} async-done(((f32[768,1152]{1,0:T(8,128)}), f32[48,1152]{1,0:T(8,128)}) %reduce-scatter.18.cloned.1.call-update) | async-done | bytes 221200 | tf_op jit(solution)/shard_map/reduce_scatter | solution.py:148
  (211 shorter events, 175.0 us)
Async XLA Ops:
  7.2 40.9 %copy-start = (bf16[768,1152]{1,0:T(8,128)(2,1)S(1)}, bf16[768,1152]{1,0:T(8,128)(2,1)}, u32[]{:S(2)}) copy-start(bf16[768,1152]{1,0:T(8,128)(2,1)} %param.16) | copy-start | bytes 5308420
  7.2 35.0 %all-gather.6.cloned.1.call-start = ((), (), s32[]{:S(2)}) async-start(), calls=%async_computation.10 | async-start | bytes 2709504 | tf_op jit(solution)/shard_map/all_gather | solution.py:112
  7.9 63.1 %all-gather.8.cloned.1.call-start = ((), (), s32[]{:S(2)}) async-start(), calls=%async_computation.11 | async-start | bytes 5419008 | tf_op jit(solution)/shard_map/all_gather | solution.py:134
  42.2 37.2 %all-gather.4.cloned.1.call-start = ((), (), s32[]{:S(2)}) async-start(), calls=%async_computation.7 | async-start | bytes 5419008 | tf_op jit(solution)/shard_map/all_gather | solution.py:102
  48.0 212.2 %reduce-scatter.16.cloned.1.call-start = ((), (), s32[]{:S(2)}) async-start(), calls=%async_computation.12 | async-start | bytes 5419008 | tf_op jit(solution)/shard_map/reduce_scatter | solution.py:139
  55.0 6.6 %copy-start.9 = (f32[1176,6]{0,1:T(8,128)}, f32[1176,6]{0,1:T(8,128)S(1)}, u32[]{:S(2)}) copy-start(f32[1176,6]{0,1:T(8,128)S(1)} %broadcast_multiply_fusion.4) | copy-start | bytes 84676
  55.1 6.6 copy-start.24
  55.1 6.6 copy-start.11
  70.3 9.0 %copy-start.3 = (bf16[6,1,1176,64]{2,3,1,0:T(8,128)(2,1)}, bf16[6,1,1176,64]{2,3,1,0:T(8,128)(2,1)S(1)}, u32[]{:S(2)}) copy-start(bf16[6,1,1176,64]{2,3,1,0:T(8,128)(2,1)S(1)} %fusion.75) | copy-start | bytes 2709508
  79.3 13.2 %copy-start.29 = (bf16[768,768]{1,0:T(8,128)(2,1)S(1)}, bf16[768,768]{1,0:T(8,128)(2,1)}, u32[]{:S(2)}) copy-start(bf16[768,768]{1,0:T(8,128)(2,1)} %param.19) | copy-start | bytes 3538948
  97.1 170.2 %reduce-scatter.12.cloned.1.call-start = ((), (), s32[]{:S(2)}) async-start(), calls=%async_computation.8 | async-start | bytes 5419008 | tf_op jit(solution)/shard_map/reduce_scatter | solution.py:105
  98.3 34.2 %copy-start.17 = (bf16[768,384]{1,0:T(8,128)(2,1)S(1)}, bf16[768,384]{1,0:T(8,128)(2,1)}, u32[]{:S(2)}) copy-start(bf16[768,384]{1,0:T(8,128)(2,1)} %param.18) | copy-start | bytes 1769476
  147.9 183.6 %reduce-scatter.24.cloned.1.call-start = ((), (), s32[]{:S(2)}) async-start(), calls=%async_computation.17 | async-start | bytes 1327104
  239.8 131.1 %reduce-scatter.20.cloned.1.call-start = ((), (), s32[]{:S(2)}) async-start(), calls=%async_computation.15 | async-start | bytes 1327104 | tf_op jit(solution)/shard_map/reduce_scatter | solution.py:153
  240.3 7.4 %copy-start.28 = (bf16[2352,768]{1,0:T(8,128)(2,1)S(1)}, bf16[2352,768]{1,0:T(8,128)(2,1)}, u32[]{:S(2)}) copy-start(bf16[2352,768]{1,0:T(8,128)(2,1)} %all-gather.4.cloned.1.call-done) | copy-start | bytes 10838020
  240.3 7.4 %copy-start.32 = (bf16[2352,768]{1,0:T(8,128)(2,1)S(1)}, bf16[2352,768]{1,0:T(8,128)(2,1)}, u32[]{:S(2)}) copy-start(bf16[2352,768]{1,0:T(8,128)(2,1)} %copy-done.31) | copy-start | bytes 10838020
  252.2 216.0 %all-reduce.3.cloned.1.call-start = ((), (), s32[]{:S(2)}) async-start(), calls=%async_computation.13 | async-start | bytes 7225344 | tf_op jit(solution)/shard_map/psum | solution.py:142
  267.3 251.8 %reduce-scatter.14.cloned.1.call-start = ((), (), s32[]{:S(2)}) async-start(), calls=%async_computation.9 | async-start | bytes 5419008 | tf_op jit(solution)/shard_map/reduce_scatter | solution.py:108
  273.0 308.2 %reduce-scatter.22.cloned.1.call-start = ((), (), s32[]{:S(2)}) async-start(), calls=%async_computation.16 | async-start | bytes 1253376
  279.2 373.6 %reduce-scatter.18.cloned.1.call-start = ((), (), s32[]{:S(2)}) async-start(), calls=%async_computation.14 | async-start | bytes 3760128 | tf_op jit(solution)/shard_map/reduce_scatter | solution.py:148
  286.4 5.0 copy-start.26
  286.4 181.7 %copy-start.19 = (f32[1176]{0:T(1024)S(1)}, f32[1176]{0:T(1024)}, u32[]{:S(2)}) copy-start(f32[1176]{0:T(1024)} %copy-done.18) | copy-start | bytes 14116
  286.4 181.7 %copy-start.21 = (f32[1176]{0:T(1024)S(1)}, f32[1176]{0:T(1024)}, u32[]{:S(2)}) copy-start(f32[1176]{0:T(1024)} %copy-done.20) | copy-start | bytes 14116
  286.5 181.7 %copy-start.23 = (f32[768]{0:T(1024)S(1)}, f32[768]{0:T(1024)}, u32[]{:S(2)}) copy-start(f32[768]{0:T(1024)} %copy-done.22) | copy-start | bytes 9220
  (20 other events, 49.4 us)
Sparse Core Ops, SparseCore 0:
  9.6 32.5 all-gather.5
  43.7 12.8 all-gather.7
  58.7 13.9 all-gather.3
  97.2 11.6 reduce-scatter.15
  148.0 11.8 reduce-scatter.11
  239.9 64.4 reduce-scatter.23
  307.8 63.0 reduce-scatter.19
  373.2 94.9 all-reduce.2
  470.4 48.6 reduce-scatter.13
  523.1 57.9 reduce-scatter.21
  585.6 67.1 reduce-scatter.17
where the time goes:
time: 666 us; the launch traced here: 659 us
  waiting for transfers between devices  307 us (46%)
  matrix products  178 us (27%)
  blocking collectives  73.3 us (11%)
  other arithmetic  52.7 us (8%)
  local copies, waits for them, and re-layouts  31.3 us (5%)
  between operations  15.9 us (2%)
    psum x1, waiting for transfers between devices, shards(): grad_normed = lax.psum(grad_normed_att + grad_normed_mlp, 'hg')  95.6 us
    reduce_scatter x1, waiting for transfers between devices, shards(): lax.psum_scatter(grad_w_qkv, ('dp', 'hid'), scatter_dimension=0, tiled=True)  71.6 us
    unnamed x13, waiting for transfers between devices  59.8 us
    psum x1, blocking collectives, shards(): qk_gains_grad = lax.psum(qk_partial, ('dp', 'hg', 'hid'))  40.1 us
    reduce_scatter x1, waiting for transfers between devices, shards(): lax.psum_scatter(grad_w_in.astype(jnp.bfloat16), 'dp', scatter_dimension=...  37.4 us
    all_gather x1, waiting for transfers between devices, shards(): grad_out = lax.all_gather(cotangent, 'hg', axis=1, tiled=True)  34.2 us
    unnamed x1, blocking collectives  33.2 us
    dot_general x12, matrix products, masked_scores(): jnp.einsum('gqe,gke->gqk', queries, keys_in, preferred_element_type=jnp.f...  32.3 us
  transfers between devices with their start and end apart: 11, of which 6 were waited for; matrix products, arithmetic and copies ran while one was open for 36% of the time, Pallas kernels for 0%

commit v1 on v0

--- a/solution.py
+++ b/solution.py
@@ -5,6 +5,18 @@
 
 PATCHES = 196
 EPSILON = 1e-06
+
+
+def doubled_up(x, axis, dim):
+    ways, here = (lax.axis_size(axis), lax.axis_index(axis))
+    grown, reach = (x, 1)
+    while reach < ways:
+        theirs = lax.ppermute(grown, axis, [(d, d ^ reach) for d in range(ways)])
+        mine_first = jnp.concatenate([grown, theirs], axis=dim)
+        theirs_first = jnp.concatenate([theirs, grown], axis=dim)
+        grown = jnp.where(here & reach == 0, mine_first, theirs_first)
+        reach = 2 * reach
+    return grown
 
 
 def normalize(values):
@@ -109,7 +121,7 @@
     out_cols = width // lax.axis_size("hg")
     input_cols = lax.dynamic_slice_in_dim(inputs, lax.axis_index("hg") * out_cols, out_cols, 1)
     output = (input_cols + mixed).astype(jnp.bfloat16)
-    grad_out = lax.all_gather(cotangent, "hg", axis=1, tiled=True)
+    grad_out = doubled_up(cotangent, "hg", 1)
     grad_w_out = rows_t(grad_out, attended_low)
     grad_attended = jnp.dot(grad_out, w_out_t, preferred_element_type=jnp.float32)
     grad_att_low = (

time: 666 us -> 647 us (0.971)
  waiting for transfers between devices: 307 us -> 284 us
  other arithmetic: 52.7 us -> 62.7 us
  local copies, waits for them, and re-layouts: 31.3 us -> 21.3 us
    reduce_scatter x0 -> x2, waiting for transfers between devices: none -> 98.4 us  [the longest x1 59.2 us: shards(): lax.psum_scatter(grad_w_out, ('dp', 'hid'), scatter_dimension=0, tiled=True)]
    unnamed x13 -> x10, waiting for transfers between devices: 59.8 us -> 0.16 us
    reduce_scatter x1, waiting for transfers between devices: 37.4 us -> 0.01 us  [shards(): lax.psum_scatter(grad_w_in.astype(jnp.bfloat16), 'dp', scatter_dimension=...]
    all_gather x1 -> x0, waiting for transfers between devices: 34.2 us -> none  [shards(): grad_out = lax.all_gather(cotangent, 'hg', axis=1, tiled=True)]
    ppermute x0 -> x1, waiting for transfers between devices: none -> 9.77 us  [doubled_up(): theirs = lax.ppermute(grown, axis, [(d, d ^ reach) for d in range(ways)])]
    unnamed x75 -> x73, local copies, waits for them, and re-layouts: 24.8 us -> 15.1 us
  transfers between devices with their start and end apart: 11 -> 11, of which waited for: 6 -> 6; matrix products, arithmetic and copies ran while one was open for 36% -> 37% of each run, Pallas kernels for 0% -> 0%
where the time goes in v1:
time: 647 us; the launch traced here: 641 us
  waiting for transfers between devices  284 us (44%)
  matrix products  178 us (28%)
  blocking collectives  74 us (11%)
  other arithmetic  62.7 us (10%)
  local copies, waits for them, and re-layouts  21.3 us (3%)
  between operations  16.1 us (2%)
    psum x1, waiting for transfers between devices, shards(): grad_normed = lax.psum(grad_normed_att + grad_normed_mlp, 'hg')  95.7 us
    reduce_scatter x1, waiting for transfers between devices, shards(): lax.psum_scatter(grad_w_qkv, ('dp', 'hid'), scatter_dimension=0, tiled=True)  71.3 us
    reduce_scatter x1, waiting for transfers between devices, shards(): lax.psum_scatter(grad_w_out, ('dp', 'hid'), scatter_dimension=0, tiled=True)  59.2 us
    psum x1, blocking collectives, shards(): qk_gains_grad = lax.psum(qk_partial, ('dp', 'hg', 'hid'))  40.8 us
    reduce_scatter x1, waiting for transfers between devices, shards(): lax.psum_scatter(grad_w_back.astype(jnp.bfloat16), 'dp', scatter_dimensio...  39.2 us
    unnamed x1, blocking collectives  33.2 us
    dot_general x12, matrix products, masked_scores(): jnp.einsum('gqe,gke->gqk', queries, keys_in, preferred_element_type=jnp.f...  32.4 us
    dot_general x4, matrix products, times_t(): lax.dot_general(left, right, (((1,), (1,)), ((), ())), preferred_element_...  25.6 us
  transfers between devices with their start and end apart: 11, of which 6 were waited for; matrix products, arithmetic and copies ran while one was open for 37% of the time, Pallas kernels for 0%

profile of v1, /device:TPU:0, one launch (start us, length us, event | category | flops | bytes accessed | tf_op | source)
XLA Modules:
  0.0 641.1 jit_solution(11084577099518265443)
XLA Ops:
  16.2 6.5 %fusion.75 = f32[1176,1152]{0,1:T(8,128)} fusion(bf16[1176,768]{1,0:T(8,128)(2,1)} %multiply_convert_fusion.2, bf16[768,1152]{1,0:T(8,128)(2,1)S(1)} %copy-done), kind=kOutput, calls=%fused_computation.141 | convolution fusion | flops 2080899072 | bytes 8994816 | tf_op jit(solution)/shard_map/dot_general | solution.py:101
  26.6 9.8 %collective-permute-done = bf16[1176,384]{1,0:T(8,128)(2,1)} collective-permute-done((bf16[1176,384]{1,0:T(8,128)(2,1)S(1)}, bf16[1176,384]{1,0:T(8,128)(2,1)}, u32[]{:S(2)}, u32[]{:S(2)}) %collective-permute-start) | collective-permute-done | bytes 903200 | tf_op jit(solution)/shard_map/ppermute | solution.py:14
  55.2 8.3 %fusion.76 = f32[2352,768]{1,0:T(8,128)} fusion(bf16[2352,768]{1,0:T(8,128)(2,1)} %all-gather.3.cloned.1.call-done, bf16[768,768]{1,0:T(8,128)(2,1)} %param.19), kind=kOutput, calls=%fused_computation.142 | convolution fusion | flops 2774532096 | bytes 12017664 | tf_op jit(solution)/shard_map/dot_general | solution.py:115
  63.5 9.4 %fusion.54 = bf16[2352,768]{1,0:T(8,128)(2,1)S(1)} fusion(f32[2352,768]{1,0:T(8,128)} %fusion.76, bf16[2352,768]{1,0:T(8,128)(2,1)} %all-gather.5.cloned.1.call-done, bf16[768,768]{1,0:T(8,128)(2,1)} %param.20), kind=kOutput, calls=%fused_computation.61 | convolution fusion | flops 2810658816 | bytes 15630336 | tf_op jit(solution)/shard_map/dot_general | solution.py:147
  74.8 4.5 convolution_convert_fusion
  80.5 33.6 %while.30 = (s32[]{:T(128)}, bf16[6,1,1176,64]{2,3,1,0:T(8,128)(2,1)S(1)}, f32[6,1,1176]{2,1,0:T(1,128)S(1)}, bf16[6,1,1176,64]{3,2,1,0:T(8,128)(2,1)}, bf16[6,1...) while((s32[]{:T(128)}, ...), condition=%wide.region_9.10_spmd.clone.clone, body=%wide.region_6.9_spmd.clone.sunk.clone | while | flops 366487456 | bytes 18392728 | solution.py:85
  120.5 9.6 %convolution_convert_fusion.1 = bf16[2352,768]{1,0:T(8,128)(2,1)} fusion(bf16[768,768]{1,0:T(8,128)(2,1)} %param.20, f32[2352,768]{1,0:T(8,128)} %fusion.76), kind=kOutput, calls=%fused_computation.64 | convolution fusion | flops 2792595456 | bytes 12017664 | tf_op jit(solution)/shard_map/dot_general | solution.py:34
  131.4 78.8 %while.31 = (s32[]{:T(128)}, f32[6,1,1176,64]{2,3,1,0:T(8,128)}, f32[6,1,1176,64]{2,3,1,0:T(8,128)}, bf16[6,1,1176,64]{2,3,1,0:T(8,128)(2,1)S(1)}, bf16[6,1,1176...) while((s32[]{:T(128)}, f32[6,1,1176,64]{2,3,1,0:T(8,128)}, ...), condition=%wide.region_14.15_spmd.clone.clone, body=%wide.region_12.14_spmd.clone.sunk.clone | while | flops 898933184 | bytes 44843632 | solution.py:85
  210.2 5.6 fusion.56
  215.9 4.4 convolution_convert_fusion.4
  224.9 8.7 %convolution_convert_fusion.3 = bf16[768,768]{1,0:T(8,128)(2,1)} fusion(bf16[2352,768]{1,0:T(8,128)(2,1)} %all-gather.5.cloned.1.call-done, f32[2352,768]{1,0:T(8,128)} %fusion.76), kind=kOutput, calls=%fused_computation.108 | convolution fusion | flops 2791378944 | bytes 12017664 | tf_op jit(solution)/shard_map/dot_general | solution.py:40
  235.2 4.1 fusion.67
  241.7 7.0 %convolution_add_fusion.1 = f32[1176,768]{1,0:T(8,128)} fusion(bf16[1176,1152]{0,1:T(8,128)(2,1)} %bitcast.271, bf16[768,1152]{1,0:T(8,128)(2,1)S(1)} %copy-done, bf16[1176,768]{1,0:T(8,128)(2,1)} %reduce-scatter.12.cloned.1.call-done), kind=kOutput, calls=%fused_computation.66 | convolution fusion | flops 2082705408 | bytes 9897984 | tf_op jit(solution)/shard_map/dot_general | solution.py:34
  249.9 4.5 convolution_add_fusion
  258.5 7.0 %fusion.77 = f32[768,1152]{1,0:T(8,128)} fusion(bf16[1176,768]{1,0:T(8,128)(2,1)} %multiply_convert_fusion.2, bf16[1176,1152]{0,1:T(8,128)(2,1)} %bitcast.272), kind=kOutput, calls=%fused_computation.143 | convolution fusion | flops 2080899072 | bytes 8054784 | tf_op jit(solution)/shard_map/dot_general | solution.py:40
  270.5 40.8 %psum.15 = f32[2,64]{1,0:T(2,128)} all-reduce(f32[2,64]{1,0:T(2,128)S(1)} %pad_maximum_fusion.1), channel_id=1, replica_groups=mesh['dp'=8,'hg'=2,'hid'=2] {'dp','hg','hid'}, use_global_device_ids=true, to_apply=%region_28.29 | all-reduce | flops 128 | bytes 1024 | tf_op jit(solution)/shard_map/psum | solution.py:172
  313.0 39.2 %reduce-scatter.20.cloned.1.call-done = bf16[96,768]{1,0:T(8,128)(2,1)} async-done(((bf16[768,768]{1,0:T(8,128)(2,1)}), bf16[96,768]{1,0:T(8,128)(2,1)}) %reduce-scatter.20.cloned.1.call-update) | async-done | bytes 147472 | tf_op jit(solution)/shard_map/reduce_scatter | solution.py:168
  353.8 95.7 %all-reduce.3.cloned.1.call-done = f32[1176,768]{1,0:T(8,128)} async-done(((f32[1176,768]{1,0:T(8,128)}), f32[1176,768]{1,0:T(8,128)}) %all-reduce.3.cloned.1.call-update) | async-done | bytes 3612688 | tf_op jit(solution)/shard_map/psum | solution.py:154
  449.5 4.1 multiply_reduce_fusion.1
  453.6 33.2 %all-reduce = f32[768]{0:T(1024)S(1)} all-reduce(f32[768]{0:T(1024)S(1)} %get-tuple-element.216), channel_id=5, replica_groups=mesh['dp'=8,'hg'=2,'hid'=2] {'dp','hid'}, use_global_device_ids=true, to_apply=%region_24.25.clone | all-reduce | flops 768 | bytes 6144
  487.4 4.7 add_convert_fusion
  492.1 8.4 %reduce-scatter.10.cloned.1.call-done = f32[1176,384]{1,0:T(8,128)} async-done(((f32[1176,768]{1,0:T(8,128)}), f32[1176,384]{1,0:T(8,128)}) %reduce-scatter.10.cloned.1.call-update) | async-done | bytes 1806352 | tf_op jit(solution)/shard_map/reduce_scatter | solution.py:120
  503.6 59.2 %reduce-scatter.16.cloned.1.call-done = f32[48,384]{1,0:T(8,128)} async-done(((f32[768,384]{1,0:T(8,128)}), f32[48,384]{1,0:T(8,128)}) %reduce-scatter.16.cloned.1.call-update) | async-done | bytes 73744 | tf_op jit(solution)/shard_map/reduce_scatter | solution.py:161
  562.8 71.3 %reduce-scatter.14.cloned.1.call-done = f32[48,1152]{1,0:T(8,128)} async-done(((f32[768,1152]{1,0:T(8,128)}), f32[48,1152]{1,0:T(8,128)}) %reduce-scatter.14.cloned.1.call-update) | async-done | bytes 221200 | tf_op jit(solution)/shard_map/reduce_scatter | solution.py:160
  (210 shorter events, 178.5 us)
Async XLA Ops:
  7.2 9.0 %copy-start = (bf16[768,1152]{1,0:T(8,128)(2,1)S(1)}, bf16[768,1152]{1,0:T(8,128)(2,1)}, u32[]{:S(2)}) copy-start(bf16[768,1152]{1,0:T(8,128)(2,1)} %param.16) | copy-start | bytes 5308420
  7.2 48.0 %all-gather.3.cloned.1.call-start = ((), (), s32[]{:S(2)}) async-start(), calls=%async_computation.7 | async-start | bytes 5419008 | tf_op jit(solution)/shard_map/all_gather | solution.py:114
  13.1 50.4 %all-gather.5.cloned.1.call-start = ((), (), s32[]{:S(2)}) async-start(), calls=%async_computation.10 | async-start | bytes 5419008 | tf_op jit(solution)/shard_map/all_gather | solution.py:146
  13.2 23.2 %collective-permute-start = (bf16[1176,384]{1,0:T(8,128)(2,1)S(1)}, bf16[1176,384]{1,0:T(8,128)(2,1)}, u32[]{:S(2)}, u32[]{:S(2)}) collective-permute-start(bf16[1176,384]{1,0:T(8,128)(2,1)S(1)} %copy-done.12), channel_id=1, source_target_pairs={{0,2},{2,0},{1,3},{3,1},{4,6},{6,4},{5,7},{7,5},{8,10},{10,8},{9,1... | collective-permute-start | bytes 2709512 | tf_op jit(solution)/shard_map/ppermute | solution.py:14
  26.6 13.5 %copy-start.28 = (bf16[2,64]{1,0:T(2,128)(2,1)S(1)}, bf16[2,64]{1,0:T(2,128)(2,1)}, u32[]{:S(2)}) copy-start(bf16[2,64]{1,0:T(2,128)(2,1)} %param.17) | copy-start | bytes 772
  26.6 16.2 %copy-start.8 = (f32[1176,6]{0,1:T(8,128)}, f32[1176,6]{0,1:T(8,128)S(1)}, u32[]{:S(2)}) copy-start(f32[1176,6]{0,1:T(8,128)S(1)} %broadcast_multiply_fusion.4) | copy-start | bytes 84676
  39.4 202.3 %reduce-scatter.12.cloned.1.call-start = ((), (), s32[]{:S(2)}) async-start(), calls=%async_computation.11 | async-start | bytes 5419008 | tf_op jit(solution)/shard_map/reduce_scatter | solution.py:151
  63.5 11.3 %copy-start.30 = (bf16[768,768]{1,0:T(8,128)(2,1)S(1)}, bf16[768,768]{1,0:T(8,128)(2,1)}, u32[]{:S(2)}) copy-start(bf16[768,768]{1,0:T(8,128)(2,1)} %param.19) | copy-start | bytes 3538948
  79.4 169.5 %reduce-scatter.8.cloned.1.call-start = ((), (), s32[]{:S(2)}) async-start(), calls=%async_computation.8 | async-start | bytes 5419008 | tf_op jit(solution)/shard_map/reduce_scatter | solution.py:117
  80.5 34.2 %copy-start.17 = (bf16[768,384]{1,0:T(8,128)(2,1)S(1)}, bf16[768,384]{1,0:T(8,128)(2,1)}, u32[]{:S(2)}) copy-start(bf16[768,384]{1,0:T(8,128)(2,1)} %param.18) | copy-start | bytes 1769476
  130.2 181.2 %reduce-scatter.18.cloned.1.call-start = ((), (), s32[]{:S(2)}) async-start(), calls=%async_computation.15 | async-start | bytes 1327104 | tf_op jit(solution)/shard_map/reduce_scatter | solution.py:165
  131.3 78.8 %copy-start.9 = (f32[1176,6]{0,1:T(8,128)S(1)}, f32[1176,6]{0,1:T(8,128)}, u32[]{:S(2)}) copy-start(f32[1176,6]{0,1:T(8,128)} %copy-done.8) | copy-start | bytes 84676
  131.3 78.8 %copy-start.11 = (f32[1176,6]{0,1:T(8,128)S(1)}, f32[1176,6]{0,1:T(8,128)}, u32[]{:S(2)}) copy-start(f32[1176,6]{0,1:T(8,128)} %copy-done.10) | copy-start | bytes 84676
  131.3 78.8 %copy-start.14 = (f32[1176,6]{0,1:T(8,128)S(1)}, f32[1176,6]{0,1:T(8,128)}, u32[]{:S(2)}) copy-start(f32[1176,6]{0,1:T(8,128)} %copy-done.13) | copy-start | bytes 84676
  131.3 78.8 %copy-start.16 = (f32[1176,6]{0,1:T(8,128)S(1)}, f32[1176,6]{0,1:T(8,128)}, u32[]{:S(2)}) copy-start(f32[1176,6]{0,1:T(8,128)} %copy-done.15) | copy-start | bytes 84676
  131.3 78.8 %copy-start.25 = (f32[64]{0:T(128)S(1)}, f32[64]{0:T(128)}, u32[]{:S(2)}) copy-start(f32[64]{0:T(128)} %copy-done.24) | copy-start | bytes 772
  220.3 131.9 %reduce-scatter.20.cloned.1.call-start = ((), (), s32[]{:S(2)}) async-start(), calls=%async_computation.16 | async-start | bytes 1327104 | tf_op jit(solution)/shard_map/reduce_scatter | solution.py:168
  233.6 215.9 %all-reduce.3.cloned.1.call-start = ((), (), s32[]{:S(2)}) async-start(), calls=%async_computation.12 | async-start | bytes 7225344 | tf_op jit(solution)/shard_map/psum | solution.py:154
  248.8 251.7 %reduce-scatter.10.cloned.1.call-start = ((), (), s32[]{:S(2)}) async-start(), calls=%async_computation.9 | async-start | bytes 5419008 | tf_op jit(solution)/shard_map/reduce_scatter | solution.py:120
  254.5 308.3 %reduce-scatter.16.cloned.1.call-start = ((), (), s32[]{:S(2)}) async-start(), calls=%async_computation.14 | async-start | bytes 1253376 | tf_op jit(solution)/shard_map/reduce_scatter | solution.py:161
  258.3 375.8 %reduce-scatter.14.cloned.1.call-start = ((), (), s32[]{:S(2)}) async-start(), calls=%async_computation.13 | async-start | bytes 3760128 | tf_op jit(solution)/shard_map/reduce_scatter | solution.py:160
  265.5 184.0 %copy-start.19 = (f32[1176]{0:T(1024)S(1)}, f32[1176]{0:T(1024)}, u32[]{:S(2)}) copy-start(f32[1176]{0:T(1024)} %copy-done.18) | copy-start | bytes 14116
  265.5 184.0 %copy-start.21 = (f32[1176]{0:T(1024)S(1)}, f32[1176]{0:T(1024)}, u32[]{:S(2)}) copy-start(f32[1176]{0:T(1024)} %copy-done.20) | copy-start | bytes 14116
  265.5 184.0 %copy-start.23 = (f32[768]{0:T(1024)S(1)}, f32[768]{0:T(1024)}, u32[]{:S(2)}) copy-start(f32[768]{0:T(1024)} %copy-done.22) | copy-start | bytes 9220
  (21 other events, 71.2 us)
Sparse Core Ops, SparseCore 0:
  13.3 15.4 all-gather.2
  39.6 14.2 all-gather.4
  79.5 12.9 reduce-scatter.11
  130.3 12.9 reduce-scatter.7
  220.4 65.6 reduce-scatter.17
  289.3 62.8 reduce-scatter.19
  354.5 94.9 all-reduce.2
  451.8 48.6 reduce-scatter.9
  504.7 58.0 reduce-scatter.15
  567.1 66.9 reduce-scatter.13
